TPU v7x, 32 devices: a whole 2x2x4 slice. The times are simulated.
32 devices in a mesh: users: 8 (over z, x), items: 4 (over y, core).
Axes of the slice: x: 2, y: 2, z: 4, core: 2. Of those that a mesh axis runs over, the one named last changes fastest.
Arguments:
- tile_users: int32 [8, 4, 128], P('users', 'items'), may hold values from 0 to 127
- tile_owners: int32 [8, 4, 128, 1], P('users', 'items'), may hold values from 0 to 7; in each aligned block of 128 rows (0 to 127, 128 to 255, ..., all dimensions but the last counted through in order) at most 32 rows name the same one
- tile_blocks: int32 [8, 4, 128], P('users', 'items'), may hold values from 0 to 63
- tile_contexts: int32 [8, 4, 128], P('users', 'items'), may hold values from 0 to 7
- row_users: int32 [8, 4, 128, 128], P('users', 'items'), may hold values from 0 to 15
- row_items: int32 [8, 4, 128, 128], P('users', 'items'), may hold values from 0 to 15
- row_contexts: int32 [8, 4, 128, 128], P('users', 'items'), may hold values from 0 to 127
- tile_values: bfloat16 [8, 4, 128, 128], P('users', 'items'), may hold values from -49152 to 49152
- tile_count: int32 [8, 4], P('users', 'items'), may hold values from 64 to 128, as said below
- item_factors: bfloat16 [8192, 256], P('users'), may hold values from -0.125 to 0.25
- context_factors: bfloat16 [1024, 256], replicated, may hold values from -0.125 to 0.25
- profile: bfloat16 [16384, 2048], P('users', 'items'), may hold values from -192 to 192
- feature_factors: bfloat16 [2048, 256], P('items'), may hold values from -6 to 6
Outputs:
- user_factors: bfloat16 [16384, 256], P('users')
- feature_new: bfloat16 [2048, 256], P('items')
Inputs may be any that keep to these rules, and one draw needn't show every extreme that they name: On one device at most 32 tiles name one index of users in tile_owners, a bound that some block reaches. The live tiles of a device are its first tile_count tiles; some device has all 128 live.
All inputs are finite; a program needn't handle non-finite values.
Results may differ from a plain program's by a relative error of at most 0.00155.
The roundings to bfloat16 on the way count: a program that leaves them out, or rounds other values in their place, can miss the bound.
Values may be sent and summed in bfloat16 or wider, within the bound.
No kernel may reach another device: no remote copies, remote signals or barrier semaphores. Data moves between devices by JAX's collectives and lax.ppermute only.
A program may use at most 64 MiB of HBM per device.

v0:
```python
import jax
import jax.numpy as jnp
from jax import lax
from jax.sharding import PartitionSpec as P

CB = 128
IB = 16
UB = 16
RIDGE = 1.0


def gram(matrix):
    return lax.dot_general(
        matrix, matrix, (((0,), (0,)), ((), ())), preferred_element_type=jnp.float32
    )


def solve_rows(normal, right_side):
    cholesky_factor = jnp.linalg.cholesky(normal)
    return jax.scipy.linalg.cho_solve((cholesky_factor, True), right_side.T).T


def local(
    tile_users,
    tile_owners,
    tile_blocks,
    tile_contexts,
    row_users,
    row_items,
    row_contexts,
    tile_values,
    tile_count,
    item_factors,
    context_factors,
    profile,
    feature_factors,
):
    users_size = lax.axis_size("users")
    tile_total = tile_users.shape[2]
    rank_width = item_factors.shape[1]
    slab_users = profile.shape[0]
    blocks_held = item_factors.shape[0] // IB
    capacity = max(2, 2 * tile_total // users_size)
    owners = tile_owners.reshape(tile_total)
    local_block = tile_blocks.reshape(tile_total)
    live_count = tile_count.reshape(())
    position = jnp.arange(tile_total, dtype=jnp.int32)
    same_owner = (owners[:, None] == owners[None, :]) & (position[None, :] < position[:, None])
    slot_rank = jnp.sum(same_owner.astype(jnp.int32), axis=1)
    tile_place = owners * capacity + slot_rank
    request_block = jnp.where(position < live_count, local_block, 0)
    wanted = jnp.zeros((users_size * capacity,), jnp.int32).at[tile_place].set(request_block)
    asked_blocks = lax.all_to_all(
        wanted.reshape(users_size, capacity), "users", split_axis=0, concat_axis=0, tiled=True
    )
    shard_blocks = item_factors.reshape(blocks_held, IB, rank_width)
    answered = shard_blocks[asked_blocks.reshape(-1)].reshape(users_size, capacity, IB, rank_width)
    fetched = lax.all_to_all(answered, "users", split_axis=0, concat_axis=0, tiled=True).reshape(
        users_size * capacity, IB, rank_width
    )
    identity = jnp.eye(rank_width, dtype=jnp.float32)
    context_gram = gram(context_factors)
    item_gram = lax.psum(gram(item_factors), "users")
    feature_gram = lax.psum(gram(feature_factors), "items")
    normal = item_gram * context_gram + feature_gram
    normal = normal + RIDGE * identity
    user_blocks = slab_users // UB
    context_table = context_factors.reshape(-1, CB, rank_width)
    tile_ublock = tile_users.reshape(tile_total)
    tile_cblock = tile_contexts.reshape(tile_total)
    users_rows = row_users.reshape(tile_total, -1)
    items_rows = row_items.reshape(tile_total, -1)
    contexts_rows = row_contexts.reshape(tile_total, -1)
    values_rows = tile_values.reshape(tile_total, -1)
    group_size = 16

    def add_group(step_index, running):
        first_tile = step_index * group_size

        def window(source):
            return lax.dynamic_slice_in_dim(source, first_tile, group_size, 0)

        item_blocks = fetched[window(tile_place)]
        context_blocks = context_table[window(tile_cblock)]
        item_onehot = (
            window(items_rows)[:, :, None] == jnp.arange(IB, dtype=jnp.int32)[None, None, :]
        ).astype(jnp.bfloat16)
        context_onehot = (
            window(contexts_rows)[:, :, None] == jnp.arange(CB, dtype=jnp.int32)[None, None, :]
        ).astype(jnp.bfloat16)
        item_rows_sel = jnp.einsum(
            "gti,gir->gtr", item_onehot, item_blocks, preferred_element_type=jnp.float32
        )
        context_rows_sel = jnp.einsum(
            "gtc,gcr->gtr", context_onehot, context_blocks, preferred_element_type=jnp.float32
        )
        alive_mask = (first_tile + jnp.arange(group_size, dtype=jnp.int32) < live_count).astype(
            jnp.float32
        )
        weighted = window(values_rows).astype(jnp.float32) * alive_mask[:, None]
        row_terms = weighted[:, :, None] * item_rows_sel * context_rows_sel
        user_onehot = (
            window(users_rows)[:, None, :] == jnp.arange(UB, dtype=jnp.int32)[None, :, None]
        ).astype(jnp.float32)
        per_tile = jnp.einsum(
            "gut,gtr->gur", user_onehot, row_terms, precision=lax.Precision.HIGHEST
        )
        block_onehot = (
            window(tile_ublock)[None, :] == jnp.arange(user_blocks, dtype=jnp.int32)[:, None]
        ).astype(jnp.float32)
        return running + jnp.einsum(
            "bg,gur->bur", block_onehot, per_tile, precision=lax.Precision.HIGHEST
        )

    rounds = (live_count + group_size - 1) // group_size
    mttkrp = lax.fori_loop(
        0, rounds, add_group, jnp.zeros((user_blocks, UB, rank_width), jnp.float32)
    ).reshape(slab_users, rank_width)
    local_right = mttkrp + jnp.dot(profile, feature_factors, preferred_element_type=jnp.float32)
    right_side = lax.psum(local_right, "items")
    user_factors = solve_rows(normal, right_side).astype(jnp.bfloat16)
    feature_terms = lax.dot_general(
        profile, user_factors, (((0,), (0,)), ((), ())), preferred_element_type=jnp.float32
    )
    user_gram, feature_right = lax.psum((gram(user_factors), feature_terms), "users")
    feature_new = solve_rows(user_gram + RIDGE * identity, feature_right).astype(jnp.bfloat16)
    return (user_factors, feature_new)


def solution(mesh):
    in_specs = (
        P("users", "items", None),
        P("users", "items", None, None),
        P("users", "items", None),
        P("users", "items", None),
        P("users", "items", None, None),
        P("users", "items", None, None),
        P("users", "items", None, None),
        P("users", "items", None, None),
        P("users", "items"),
        P("users", None),
        P(),
        P("users", "items"),
        P("items", None),
    )
    out_specs = (P("users", None), P("items", None))
    return jax.shard_map(local, mesh=mesh, in_specs=in_specs, out_specs=out_specs, check_vma=False)
```

profile of v0, /device:TPU:0, one launch (start us, length us, event | category | flops | bytes accessed | tf_op | source)
XLA Modules:
  0.0 481.4 jit_solution(13912460111386983107)
XLA Ops:
  11.3 13.6 %all_to_all.14 = s32[8,1,32]{2,1,0:T(1,128)S(1)} all-to-all(s32[8,1,32]{2,1,0:T(1,128)S(1)} %all_to_all.9), channel_id=1, replica_groups=mesh['users'=8,'items'=4] {'users'}, dimensions={0} | all-to-all | bytes 2048 | tf_op jit(solution)/shard_map/all_to_all | solution.py:53
  26.1 3.1 gather_fusion.2
  29.2 4.5 all-to-all-start.1
  35.9 48.9 %all-to-all-done.1 = bf16[8,32,16,256]{3,2,1,0:T(8,128)(2,1)} async-done(((bf16[8,32,16,256]{3,2,1,0:T(8,128)(2,1)}), bf16[8,32,16,256]{3,2,1,0:T(8,128)(2,1)}, u32[]{:S(2)}, u32[]{:S(2)}) %all-to-all-start.1) | async-done | bytes 2097184 | tf_op jit(solution)/shard_map/all_to_all | solution.py:58
  86.4 115.0 %while.12 = (s32[]{:T(128)}, f32[128,16,256]{2,0,1:T(8,128)}, s32[]{:T(128)}, s32[128]{0:T(128)S(1)}, s32[128,128]{1,0:T(8,128)}, /*index=5*/bf16[128,128]{1,0:T...) while((s32[]{:T(128)}, f32[128,16,256]{2,0,1:T(8,128)}, ...), condition=%wide.region_9.11_spmd, body=%wide.region_8.10_spmd.sunk | while | flops 354230400 | bytes 25138244 | solution.py:116
  90.6 2.1 gather_fusion.1
  96.7 4.0 convolution_add_fusion.3
  111.1 4.0 convolution_add_fusion.3
  119.4 2.1 gather_fusion.1
  125.5 4.0 convolution_add_fusion.3
  133.8 2.1 gather_fusion.1
  139.9 4.0 convolution_add_fusion.3
  148.2 2.1 gather_fusion.1
  154.3 4.0 convolution_add_fusion.3
  168.6 4.0 convolution_add_fusion.3
  176.9 2.1 gather_fusion.1
  183.0 4.0 convolution_add_fusion.3
  197.4 4.0 convolution_add_fusion.3
  201.4 2.8 copy.28
  206.9 54.0 %all-reduce.11.cloned.1.call-done = (f32[256,2048]{0,1:T(8,128)}, f32[256,256]{0,1:T(8,128)}) async-done(((f32[256,2048]{0,1:T(8,128)}, f32[256,256]{0,1:T(8,128)}), (f32[256,2048]{0,1:T(8,128)}, f32[256,256]{0,1:T(8,128)})) %all-reduce.11.cloned.1.call-update) | async-done | bytes 2359312 | tf_op jit(solution)/shard_map/psum | solution.py:120
  262.5 11.7 %cholesky.130 = f32[128,128]{1,0:T(8,128)S(1)} custom-call(f32[128,128]{1,0:T(8,128)S(1)} %cholesky.194), custom_call_target="Cholesky" | custom-call | tf_op jit(solution)/shard_map/jit(cholesky)/cholesky | solution.py:19
  274.3 9.8 %custom-call.25 = f32[1,128,128]{1,2,0:T(8,128)S(1)} custom-call(f32[1,128,128]{2,1,0:T(8,128)S(1)} %get-tuple-element.153), custom_call_target="InvertDiagBlocksLowerTriangular" | custom-call | tf_op jit(solution)/shard_map/jit(cholesky)/cholesky | solution.py:19
  284.6 11.7 %cholesky.147 = f32[128,128]{1,0:T(8,128)S(1)} custom-call(f32[128,128]{1,0:T(8,128)S(1)} %convolution_subtract_fusion.5), custom_call_target="Cholesky" | custom-call | tf_op jit(solution)/shard_map/jit(cholesky)/cholesky | solution.py:19
  298.4 4.2 while.13
  302.6 19.7 %custom-call.22 = f32[2,128,128]{1,2,0:T(8,128)S(1)} custom-call(f32[2,128,128]{2,1,0:T(8,128)S(1)} %get-tuple-element.79), custom_call_target="InvertDiagBlocksLowerTriangular" | custom-call | tf_op jit(solution)/shard_map/jit(_cho_solve)/triangular_solve | solution.py:20
  322.2 2.4 fusion.16
  336.2 72.6 %all-reduce.9.cloned.1.call-done = (f32[256,512]{1,0:T(8,128)}, f32[256,256]{0,1:T(8,128)}) async-done(((f32[256,512]{1,0:T(8,128)}, f32[256,256]{0,1:T(8,128)}), (f32[256,512]{1,0:T(8,128)}, f32[256,256]{0,1:T(8,128)})) %all-reduce.9.cloned.1.call-update) | async-done | bytes 786448 | tf_op jit(solution)/shard_map/psum | solution.py:125
  411.0 11.7 %cholesky.164 = f32[128,128]{1,0:T(8,128)S(1)} custom-call(f32[128,128]{1,0:T(8,128)S(1)} %cholesky.197), custom_call_target="Cholesky" | custom-call | tf_op jit(solution)/shard_map/jit(cholesky)/cholesky | solution.py:19
  422.8 9.8 %custom-call.26 = f32[1,128,128]{1,2,0:T(8,128)S(1)} custom-call(f32[1,128,128]{2,1,0:T(8,128)S(1)} %get-tuple-element.149), custom_call_target="InvertDiagBlocksLowerTriangular" | custom-call | tf_op jit(solution)/shard_map/jit(cholesky)/cholesky | solution.py:19
  433.1 11.7 %cholesky.181 = f32[128,128]{1,0:T(8,128)S(1)} custom-call(f32[128,128]{1,0:T(8,128)S(1)} %convolution_subtract_fusion.4), custom_call_target="Cholesky" | custom-call | tf_op jit(solution)/shard_map/jit(cholesky)/cholesky | solution.py:19
  447.5 3.9 while.14
  451.4 19.9 %custom-call.23 = f32[2,128,128]{1,2,0:T(8,128)S(1)} custom-call(f32[2,128,128]{2,1,0:T(8,128)S(1)} %get-tuple-element.87), custom_call_target="InvertDiagBlocksLowerTriangular" | custom-call | tf_op jit(solution)/shard_map/jit(_cho_solve)/triangular_solve | solution.py:20
  (215 shorter events, 112.3 us)
Async XLA Ops:
  7.2 197.0 %copy-start = (bf16[2048,512]{1,0:T(8,128)(2,1)S(1)}, bf16[2048,512]{1,0:T(8,128)(2,1)}, u32[]{:S(2)}) copy-start(bf16[2048,512]{1,0:T(8,128)(2,1)} %param.27) | copy-start | bytes 6291460
  29.2 4.6 copy-start.3
  29.2 5.7 %copy-start.10 = (s32[1,1,128,1]{2,3,1,0:T(1,128)S(1)}, s32[1,1,128,1]{2,3,1,0:T(1,128)}, u32[]{:S(2)}) copy-start(s32[1,1,128,1]{2,3,1,0:T(1,128)} %param.17) | copy-start | bytes 1540
  29.2 5.7 %copy-start.4 = (bf16[512,256]{1,0:T(8,128)(2,1)S(1)}, bf16[512,256]{1,0:T(8,128)(2,1)}, u32[]{:S(2)}) copy-start(bf16[512,256]{1,0:T(8,128)(2,1)} %param.28) | copy-start | bytes 786436
  29.2 55.6 %all-to-all-start.1 = ((bf16[8,32,16,256]{3,2,1,0:T(8,128)(2,1)}), bf16[8,32,16,256]{3,2,1,0:T(8,128)(2,1)}, u32[]{:S(2)}, u32[]{:S(2)}) async-start(bf16[8,32,16,256]{3,2,1,0:T(8,128)(2,1)} %bitcast.133), calls=%async_computation.1 | async-start | bytes 4194304 | tf_op jit(solution)/shard_map/all_to_all | solution.py:58
  33.7 52.7 %copy-start.9 = (s32[1,1,128]{2,1,0:T(1,128)S(1)}, s32[1,1,128]{2,1,0:T(1,128)}, u32[]{:S(2)}) copy-start(s32[1,1,128]{2,1,0:T(1,128)} %param.19) | copy-start | bytes 1540
  33.7 52.7 %copy-start.11 = (s32[1,1,128]{2,1,0:T(1,128)S(1)}, s32[1,1,128]{2,1,0:T(1,128)}, u32[]{:S(2)}) copy-start(s32[1,1,128]{2,1,0:T(1,128)} %param.16) | copy-start | bytes 1540
  33.7 173.2 %all-reduce.7.cloned.1.call-start = ((), (), s32[]{:S(2)}) async-start(), calls=%async_computation.2 | async-start | bytes 524288 | tf_op jit(solution)/shard_map/psum | solution.py:63
  34.8 226.1 %all-reduce.11.cloned.1.call-start = ((), (), s32[]{:S(2)}) async-start(), calls=%async_computation.4 | async-start | bytes 4718592 | tf_op jit(solution)/shard_map/psum | solution.py:120
  92.8 2.9 copy-start.1
  107.2 2.9 copy-start.1
  121.6 2.9 copy-start.1
  136.0 2.9 copy-start.1
  150.3 2.9 copy-start.1
  164.7 2.9 copy-start.1
  179.1 2.9 copy-start.1
  193.4 2.9 copy-start.1
  206.2 54.7 %copy-start.2 = (bf16[8,128,256]{2,1,0:T(8,128)(2,1)S(1)}, bf16[8,128,256]{2,1,0:T(8,128)(2,1)}, u32[]{:S(2)}) copy-start(bf16[8,128,256]{2,1,0:T(8,128)(2,1)} %get-tuple-element.400) | copy-start | bytes 1572868
  206.3 202.6 %all-reduce.9.cloned.1.call-start = ((), (), s32[]{:S(2)}) async-start(), calls=%async_computation.3 | async-start | bytes 1572864 | tf_op jit(solution)/shard_map/psum | solution.py:125
  322.2 2.5 copy-start.5
  328.6 3.3 copy-start.7
  330.7 1.2 copy-start.6
  409.8 61.5 %copy-start.8 = (f32[256,512]{1,0:T(8,128)S(1)}, f32[256,512]{1,0:T(8,128)}, u32[]{:S(2)}) copy-start(f32[256,512]{1,0:T(8,128)} %get-tuple-element.134) | copy-start | bytes 1572868
Sparse Core Ops, SparseCore 0:
  38.5 86.4 all-reduce.6
  206.4 54.4 all-reduce.10
  333.6 75.2 all-reduce.8
where the time goes:
time: 489 us; the launch traced here: 481 us
  waiting for transfers between devices  176 us (36%)
  other arithmetic  126 us (26%)
  matrix products  80.1 us (16%)
  local copies, waits for them, and re-layouts  62.1 us (13%)
  between operations  17.8 us (4%)
  blocking collectives  13.6 us (3%)
  starting transfers between devices  5.11 us (1%)
    psum x1, waiting for transfers between devices, local(): lax.psum((gram(user_factors), feature_terms), 'users')  72.6 us
    another operation x13, other arithmetic, solve_rows(): cholesky_factor = jnp.linalg.cholesky(normal)  68.6 us
    psum x1, waiting for transfers between devices, local(): right_side = lax.psum(local_right, 'items')  54 us
    all_to_all x1, waiting for transfers between devices, local(): lax.all_to_all(answered, 'users', split_axis=0, concat_axis=0, tiled=True)  48.9 us
    another operation x5, other arithmetic, solve_rows(): return jax.scipy.linalg.cho_solve((cholesky_factor, True), right_side.T).T  39.7 us
    dot_general x8, matrix products, add_group(): jnp.einsum('bg,gur->bur', block_onehot, per_tile, precision=lax.Precision...  32 us
    gather x8, local copies, waits for them, and re-layouts, add_group(): item_blocks = fetched[window(tile_place)]  17.2 us
    dot_general x8, matrix products, add_group(): jnp.einsum('gtc,gcr->gtr', context_onehot, context_blocks, preferred_elem...  14.5 us
  transfers between devices with their start and end apart: 4, of which 3 were waited for; matrix products, arithmetic and copies ran while one was open for 26% of the time, Pallas kernels for 0%

commit v1 on v0

--- a/solution.py
+++ b/solution.py
@@ -117,7 +117,11 @@
         0, rounds, add_group, jnp.zeros((user_blocks, UB, rank_width), jnp.float32)
     ).reshape(slab_users, rank_width)
     local_right = mttkrp + jnp.dot(profile, feature_factors, preferred_element_type=jnp.float32)
-    right_side = lax.psum(local_right, "items")
+    right_side = local_right
+    for hop in (1, 2):
+        right_side = right_side + lax.ppermute(
+            right_side, "items", [(dev, dev ^ hop) for dev in range(4)]
+        )
     user_factors = solve_rows(normal, right_side).astype(jnp.bfloat16)
     feature_terms = lax.dot_general(
         profile, user_factors, (((0,), (0,)), ((), ())), preferred_element_type=jnp.float32

time: 489 us -> 540 us (1.10)
  waiting for transfers between devices: 176 us -> 220 us
  other arithmetic: 126 us -> 133 us
    psum x1, waiting for transfers between devices: 0.02 us -> 75 us  [local(): item_gram = lax.psum(gram(item_factors), 'users')]
    psum x1, waiting for transfers between devices: 54 us -> 23.9 us  [local(): feature_gram = lax.psum(gram(feature_factors), 'items')]
  transfers between devices with their start and end apart: 4 -> 6, of which waited for: 3 -> 5; matrix products, arithmetic and copies ran while one was open for 26% -> 13% of each run, Pallas kernels for 0% -> 0%
where the time goes in v1:
time: 540 us; the launch traced here: 532 us
  waiting for transfers between devices  220 us (41%)
  other arithmetic  133 us (25%)
  matrix products  78.7 us (15%)
  local copies, waits for them, and re-layouts  62.2 us (12%)
  between operations  17.9 us (3%)
  blocking collectives  13.6 us (3%)
  starting transfers between devices  6.63 us (1%)
    psum x1, waiting for transfers between devices, local(): item_gram = lax.psum(gram(item_factors), 'users')  75 us
    psum x1, waiting for transfers between devices, local(): lax.psum((gram(user_factors), feature_terms), 'users')  71.8 us
    another operation x13, other arithmetic, solve_rows(): cholesky_factor = jnp.linalg.cholesky(normal)  68.6 us
    all_to_all x1, waiting for transfers between devices, local(): lax.all_to_all(answered, 'users', split_axis=0, concat_axis=0, tiled=True)  47 us
    another operation x5, other arithmetic, solve_rows(): return jax.scipy.linalg.cho_solve((cholesky_factor, True), right_side.T).T  39.7 us
    dot_general x8, matrix products, add_group(): jnp.einsum('bg,gur->bur', block_onehot, per_tile, precision=lax.Precision...  31.9 us
    psum x1, waiting for transfers between devices, local(): feature_gram = lax.psum(gram(feature_factors), 'items')  23.9 us
    gather x8, local copies, waits for them, and re-layouts, add_group(): item_blocks = fetched[window(tile_place)]  17.2 us
  transfers between devices with their start and end apart: 6, of which 5 were waited for; matrix products, arithmetic and copies ran while one was open for 13% of the time, Pallas kernels for 0%

profile of v1, /device:TPU:0, one launch (start us, length us, event | category | flops | bytes accessed | tf_op | source)
XLA Modules:
  0.0 532.0 jit_solution(13628335327575039476)
XLA Ops:
  11.3 13.6 %all_to_all.14 = s32[8,1,32]{2,1,0:T(1,128)S(1)} all-to-all(s32[8,1,32]{2,1,0:T(1,128)S(1)} %all_to_all.9), channel_id=1, replica_groups=mesh['users'=8,'items'=4] {'users'}, dimensions={0} | all-to-all | bytes 2048 | tf_op jit(solution)/shard_map/all_to_all | solution.py:53
  26.1 3.1 gather_fusion.2
  29.2 4.5 all-to-all-start.1
  33.8 47.0 %all-to-all-done.1 = bf16[8,32,16,256]{3,2,1,0:T(8,128)(2,1)} async-done(((bf16[8,32,16,256]{3,2,1,0:T(8,128)(2,1)}), bf16[8,32,16,256]{3,2,1,0:T(8,128)(2,1)}, u32[]{:S(2)}, u32[]{:S(2)}) %all-to-all-start.1) | async-done | bytes 2097184 | tf_op jit(solution)/shard_map/all_to_all | solution.py:58
  82.3 114.9 %while.12 = (s32[]{:T(128)}, f32[128,16,256]{2,0,1:T(8,128)}, s32[]{:T(128)}, s32[128]{0:T(128)S(1)}, s32[128,128]{1,0:T(8,128)}, /*index=5*/bf16[128,128]{1,0:T...) while((s32[]{:T(128)}, f32[128,16,256]{2,0,1:T(8,128)}, ...), condition=%wide.region_9.11_spmd, body=%wide.region_8.10_spmd.sunk | while | flops 354230400 | bytes 25138244 | solution.py:116
  86.6 2.1 gather_fusion.1
  92.7 4.0 convolution_add_fusion.3
  107.0 4.0 convolution_add_fusion.3
  115.3 2.1 gather_fusion.1
  121.4 4.0 convolution_add_fusion.3
  129.7 2.1 gather_fusion.1
  135.8 4.0 convolution_add_fusion.3
  150.1 4.0 convolution_add_fusion.3
  164.5 4.0 convolution_add_fusion.3
  178.9 4.0 convolution_add_fusion.3
  193.2 4.0 convolution_add_fusion.3
  197.2 2.9 copy.28
  206.7 3.8 add.137
  212.0 23.9 %all-reduce.8.cloned.1.call-done = f32[256,256]{0,1:T(8,128)} async-done(((f32[256,256]{0,1:T(8,128)}), f32[256,256]{0,1:T(8,128)}) %all-reduce.8.cloned.1.call-update) | async-done | bytes 262160 | tf_op jit(solution)/shard_map/psum | solution.py:64
  235.9 75.0 %all-reduce.6.cloned.1.call-done = f32[256,256]{0,1:T(8,128)} async-done(((f32[256,256]{0,1:T(8,128)}), f32[256,256]{0,1:T(8,128)}) %all-reduce.6.cloned.1.call-update) | async-done | bytes 262160 | tf_op jit(solution)/shard_map/psum | solution.py:63
  312.5 11.7 %cholesky.130 = f32[128,128]{1,0:T(8,128)S(1)} custom-call(f32[128,128]{1,0:T(8,128)S(1)} %cholesky.194), custom_call_target="Cholesky" | custom-call | tf_op jit(solution)/shard_map/jit(cholesky)/cholesky | solution.py:19
  324.3 9.8 %custom-call.25 = f32[1,128,128]{1,2,0:T(8,128)S(1)} custom-call(f32[1,128,128]{2,1,0:T(8,128)S(1)} %get-tuple-element.151), custom_call_target="InvertDiagBlocksLowerTriangular" | custom-call | tf_op jit(solution)/shard_map/jit(cholesky)/cholesky | solution.py:19
  334.6 11.7 %cholesky.147 = f32[128,128]{1,0:T(8,128)S(1)} custom-call(f32[128,128]{1,0:T(8,128)S(1)} %convolution_subtract_fusion.4), custom_call_target="Cholesky" | custom-call | tf_op jit(solution)/shard_map/jit(cholesky)/cholesky | solution.py:19
  348.4 4.2 while.13
  352.6 19.7 %custom-call.22 = f32[2,128,128]{1,2,0:T(8,128)S(1)} custom-call(f32[2,128,128]{2,1,0:T(8,128)S(1)} %get-tuple-element.79), custom_call_target="InvertDiagBlocksLowerTriangular" | custom-call | tf_op jit(solution)/shard_map/jit(_cho_solve)/triangular_solve | solution.py:20
  372.3 2.5 add_bitcast_fusion
  387.5 71.8 %all-reduce.10.cloned.1.call-done = (f32[256,512]{1,0:T(8,128)}, f32[256,256]{0,1:T(8,128)}) async-done(((f32[256,512]{1,0:T(8,128)}, f32[256,256]{0,1:T(8,128)}), (f32[256,512]{1,0:T(8,128)}, f32[256,256]{0,1:T(8,128)})) %all-reduce.10.cloned.1.call-update) | async-done | bytes 786448 | tf_op jit(solution)/shard_map/psum | solution.py:129
  461.4 11.7 %cholesky.164 = f32[128,128]{1,0:T(8,128)S(1)} custom-call(f32[128,128]{1,0:T(8,128)S(1)} %cholesky.197), custom_call_target="Cholesky" | custom-call | tf_op jit(solution)/shard_map/jit(cholesky)/cholesky | solution.py:19
  473.2 9.8 %custom-call.26 = f32[1,128,128]{1,2,0:T(8,128)S(1)} custom-call(f32[1,128,128]{2,1,0:T(8,128)S(1)} %get-tuple-element.147), custom_call_target="InvertDiagBlocksLowerTriangular" | custom-call | tf_op jit(solution)/shard_map/jit(cholesky)/cholesky | solution.py:19
  483.5 11.7 %cholesky.181 = f32[128,128]{1,0:T(8,128)S(1)} custom-call(f32[128,128]{1,0:T(8,128)S(1)} %convolution_subtract_fusion.3), custom_call_target="Cholesky" | custom-call | tf_op jit(solution)/shard_map/jit(cholesky)/cholesky | solution.py:19
  497.9 4.0 while.14
  501.9 19.9 %custom-call.23 = f32[2,128,128]{1,2,0:T(8,128)S(1)} custom-call(f32[2,128,128]{2,1,0:T(8,128)S(1)} %get-tuple-element.87), custom_call_target="InvertDiagBlocksLowerTriangular" | custom-call | tf_op jit(solution)/shard_map/jit(_cho_solve)/triangular_solve | solution.py:20
  (219 shorter events, 121.0 us)
Async XLA Ops:
  7.2 192.9 %copy-start = (bf16[2048,512]{1,0:T(8,128)(2,1)S(1)}, bf16[2048,512]{1,0:T(8,128)(2,1)}, u32[]{:S(2)}) copy-start(bf16[2048,512]{1,0:T(8,128)(2,1)} %param.27) | copy-start | bytes 6291460
  29.2 4.6 copy-start.9
  29.2 51.6 %all-to-all-start.1 = ((bf16[8,32,16,256]{3,2,1,0:T(8,128)(2,1)}), bf16[8,32,16,256]{3,2,1,0:T(8,128)(2,1)}, u32[]{:S(2)}, u32[]{:S(2)}) async-start(bf16[8,32,16,256]{3,2,1,0:T(8,128)(2,1)} %bitcast.132), calls=%async_computation.1 | async-start | bytes 4194304 | tf_op jit(solution)/shard_map/all_to_all | solution.py:58
  33.7 48.6 %copy-start.8 = (s32[1,1,128]{2,1,0:T(1,128)S(1)}, s32[1,1,128]{2,1,0:T(1,128)}, u32[]{:S(2)}) copy-start(s32[1,1,128]{2,1,0:T(1,128)} %param.19) | copy-start | bytes 1540
  33.7 48.6 %copy-start.10 = (s32[1,1,128]{2,1,0:T(1,128)S(1)}, s32[1,1,128]{2,1,0:T(1,128)}, u32[]{:S(2)}) copy-start(s32[1,1,128]{2,1,0:T(1,128)} %param.16) | copy-start | bytes 1540
  33.7 202.2 %all-reduce.8.cloned.1.call-start = ((), (), s32[]{:S(2)}) async-start(), calls=%async_computation.3 | async-start | bytes 524288 | tf_op jit(solution)/shard_map/psum | solution.py:64
  88.7 2.9 copy-start.1
  103.1 2.9 copy-start.1
  117.5 2.9 copy-start.1
  131.8 2.9 copy-start.1
  146.2 2.9 copy-start.1
  160.6 2.9 copy-start.1
  174.9 2.9 copy-start.1
  189.3 2.9 copy-start.1
  197.2 2.9 copy-start.4
  200.1 3.1 copy-start.3
  202.1 4.5 collective-permute-start
  203.2 107.8 %all-reduce.6.cloned.1.call-start = ((), (), s32[]{:S(2)}) async-start(), calls=%async_computation.2 | async-start | bytes 524288 | tf_op jit(solution)/shard_map/psum | solution.py:63
  204.3 255.0 %all-reduce.10.cloned.1.call-start = ((), (), s32[]{:S(2)}) async-start(), calls=%async_computation.4 | async-start | bytes 1572864 | tf_op jit(solution)/shard_map/psum | solution.py:129
  204.9 106.1 %copy-start.2 = (bf16[8,128,256]{2,1,0:T(8,128)(2,1)S(1)}, bf16[8,128,256]{2,1,0:T(8,128)(2,1)}, u32[]{:S(2)}) copy-start(bf16[8,128,256]{2,1,0:T(8,128)(2,1)} %get-tuple-element.395) | copy-start | bytes 1572868
  210.5 161.8 %collective-permute-start.1 = (f32[2048,256]{1,0:T(8,128)}, f32[2048,256]{1,0:T(8,128)}, u32[]{:S(2)}, u32[]{:S(2)}) collective-permute-start(f32[2048,256]{1,0:T(8,128)} %add.137), channel_id=1, source_target_pairs={{0,2},{1,3},{2,0},{3,1},{4,6},{5,7},{6,4},{7,5},{8,10},{9,11},{10,... | collective-permute-start | bytes 6291464 | tf_op jit(solution)/shard_map/ppermute | solution.py:122
  379.8 3.3 copy-start.6
  381.9 1.2 copy-start.5
  460.2 61.6 %copy-start.7 = (f32[256,512]{1,0:T(8,128)S(1)}, f32[256,512]{1,0:T(8,128)}, u32[]{:S(2)}) copy-start(f32[256,512]{1,0:T(8,128)} %get-tuple-element.134) | copy-start | bytes 1572868
Sparse Core Ops, SparseCore 0:
  203.3 32.6 all-reduce.7
  239.9 71.0 all-reduce.5
  384.8 74.4 all-reduce.9
